TPU v7x, 256 devices: a whole 4x4x8 slice. The times are simulated.
256 devices in a mesh: seq: 64 (over y, z, core), pool: 4 (over x).
Axes of the slice: x: 4, y: 4, z: 8, core: 2. Of those that a mesh axis runs over, the one named last changes fastest.
Arguments:
- query_rows: bfloat16 [32768, 4096], P('seq', 'pool'), may hold values from -6 to 6
- key_rows: bfloat16 [32768, 4096], P('seq', 'pool'), may hold values from -6 to 6
- value_rows: bfloat16 [32768, 4096], P('seq', 'pool'), may hold values from -6 to 6
- log_decay: float32 [32, 32768], P('pool', 'seq'), may hold values from -0.7 to 0
- residual: bfloat16 [32768, 4096], P(('seq', 'pool')), may hold values from -6 to 6
- out_weight: bfloat16 [4096, 4096], P('pool', 'seq'), may hold values from -0.09375 to 0.09375
- norm_gain: float32 [4096], replicated, may hold values from 0.5 to 1.5
- kv_weight: bfloat16 [4096, 1024], P('seq'), may hold values from -0.09375 to 0.09375
- block_table: int32 [256, 2], P(('seq', 'pool')), may hold values from 0 to 3, as said below
Outputs:
- page_cache: bfloat16 [64, 4, 2, 128, 1024], P('seq', 'pool')
Inputs may be any that keep to these rules, and one draw needn't show every extreme that they name: `block_table`: column 0 is a page's pool device, column 1 its slot there. The pages of one index of seq go to pool devices of that same index, no two to the same device and slot; one pool device receives exactly 2 of them, each other at most 2, and all 1 pages of some device go to that one.
All inputs are finite; a program needn't handle non-finite values.
Results may differ from a plain program's by a relative error of at most 0.0056.
Values may be sent and summed in bfloat16 or wider, within the bound.
A program may use at most 128 MiB of HBM per device.

v0:
```python
import jax
import jax.numpy as jnp
from jax import lax
from jax.sharding import PartitionSpec as P

HD = 128
PAGE = 128
BLK = 512


def entering(part, axis, combine, identity):
    place = lax.axis_index(axis)
    gathered = jax.tree.map(lambda a: lax.all_gather(a, axis), part)
    state = jax.tree.map(lambda a, e: jnp.zeros_like(a) + jnp.asarray(e, a.dtype), part, identity)

    def one(hop, state):
        return combine(
            state, jax.tree.map(lambda a: lax.dynamic_index_in_dim(a, hop, 0, False), gathered)
        )

    return lax.fori_loop(0, place, one, state)


def head_major(matrix, head_count):
    return matrix.reshape(BLK, head_count, HD).transpose(1, 0, 2)


def combine_states(earlier, later):
    return (earlier[0] + later[0], jnp.exp(later[0])[:, None, None] * earlier[1] + later[1])


def on_device(
    query_rows,
    key_rows,
    value_rows,
    log_decay,
    residual,
    out_weight,
    norm_gain,
    kv_weight,
    block_table,
):
    head_count = query_rows.shape[1] // HD
    lower_mask = jnp.tril(jnp.ones((BLK, BLK), dtype=bool))
    query_blk = head_major(query_rows, head_count)
    key_blk = head_major(key_rows, head_count)
    value_blk = head_major(value_rows, head_count)
    cumulative = jnp.cumsum(log_decay, axis=1)
    block_total = cumulative[:, -1]
    log_gap = jnp.where(lower_mask[None], cumulative[:, :, None] - cumulative[:, None, :], 0.0)
    products = jnp.einsum("hid,hjd->hij", query_blk, key_blk, preferred_element_type=jnp.float32)
    scores = jnp.where(lower_mask[None], products * jnp.exp(log_gap), 0.0).astype(jnp.bfloat16)
    inner = jnp.einsum("hij,hjd->hid", scores, value_blk, preferred_element_type=jnp.float32)
    weighted = (
        key_blk.astype(jnp.float32) * jnp.exp(block_total[:, None] - cumulative)[:, :, None]
    ).astype(jnp.bfloat16)
    update = jnp.einsum("hjd,hje->hde", weighted, value_blk, preferred_element_type=jnp.float32)
    query_list = [query_blk]
    inner_list = [inner]
    update_list = [update]
    cumul_list = [cumulative]
    total_list = [block_total]
    state_sum = jnp.zeros((head_count, HD, HD), jnp.float32)
    block_index = 0
    state_sum = (
        jnp.exp(total_list[block_index])[:, None, None] * state_sum + update_list[block_index]
    )
    log_sum = total_list[block_index]
    incoming = entering(
        (log_sum, state_sum),
        "seq",
        combine_states,
        (jnp.zeros_like(log_sum), jnp.zeros_like(state_sum)),
    )
    carried = incoming[1]
    block_index = 0
    outer = (
        jnp.einsum(
            "hid,hde->hie",
            query_list[block_index].astype(jnp.float32),
            carried,
            precision=lax.Precision.HIGHEST,
        )
        * jnp.exp(cumul_list[block_index])[:, :, None]
    )
    retained = inner_list[block_index] + outer
    scaled = retained * lax.rsqrt(jnp.mean(retained * retained, axis=-1, keepdims=True) + 1e-05)
    mixed_list = scaled.transpose(1, 0, 2).reshape(BLK, head_count * HD).astype(jnp.bfloat16)
    partial_value = jnp.dot(
        mixed_list,
        lax.all_gather(out_weight, "seq", axis=1, tiled=True),
        preferred_element_type=jnp.float32,
    )
    summed = lax.psum_scatter(partial_value, "pool", scatter_dimension=0, tiled=True)
    hidden = residual.astype(jnp.float32) + summed
    normed = (
        hidden * lax.rsqrt(jnp.mean(hidden * hidden, axis=-1, keepdims=True) + 1e-05) * norm_gain
    ).astype(jnp.bfloat16)
    pool_count = lax.axis_size("pool")
    pages_here = block_table.shape[0]
    slot_count = 2 * pages_here
    cache_width = kv_weight.shape[1]
    owner_ids = jnp.arange(pool_count, dtype=jnp.int32)
    slot_ids = jnp.arange(slot_count, dtype=jnp.int32)
    owner_match = block_table[:, 0][:, None] == owner_ids[None, :]
    slot_match = block_table[:, 1][:, None] == slot_ids[None, :]
    placed = jnp.logical_and(owner_match[:, :, None], slot_match[:, None, :]).astype(jnp.bfloat16)
    cache_rows = jnp.dot(
        normed,
        lax.all_gather(kv_weight, "seq", axis=0, tiled=True),
        preferred_element_type=jnp.float32,
    ).astype(jnp.bfloat16)
    own_pages = cache_rows.reshape(pages_here, PAGE, cache_width)
    outgoing = jnp.where(
        owner_match.T[:, :, None, None], own_pages[None], jnp.zeros((), jnp.bfloat16)
    )
    slot_tags = placed.transpose(1, 0, 2)
    arrived, arrived_tags = (
        lax.all_to_all(outgoing, "pool", split_axis=0, concat_axis=0, tiled=True),
        lax.all_to_all(slot_tags, "pool", split_axis=0, concat_axis=0, tiled=True),
    )
    page_cache = jnp.einsum(
        "ips,ipqc->sqc", arrived_tags, arrived, preferred_element_type=jnp.float32
    ).astype(jnp.bfloat16)
    return page_cache.reshape(1, 1, slot_count, PAGE, cache_width)


def solution(mesh):
    placed = (
        P("seq", "pool"),
        P("seq", "pool"),
        P("seq", "pool"),
        P("pool", "seq"),
        P(("seq", "pool"), None),
        P("pool", "seq"),
        P(),
        P("seq", None),
        P(("seq", "pool"), None),
    )
    return jax.shard_map(
        on_device,
        mesh=mesh,
        in_specs=placed,
        out_specs=P("seq", "pool", None, None, None),
        check_vma=False,
    )
```

profile of v0, /device:TPU:1, one launch (start us, length us, event | category | flops | bytes accessed | tf_op | source)
XLA Modules:
  0.0 455.7 jit_solution(11323797303742219468)
XLA Ops:
  6.5 0.0 copy-start
  6.5 0.0 copy-start.5
  6.5 0.0 all-gather.10.cloned.1.call-start
  6.5 2.4 reduce-window.6
  8.9 0.2 slice_reduce_fusion
  9.1 0.1 exponential_bitcast_fusion.1
  9.2 0.2 slice_reduce_fusion.1
  9.4 0.1 fusion.23
  9.5 1.5 copy.46
  11.0 0.0 copy-start.6
  11.0 0.0 copy-start.9
  11.0 0.0 copy-done.5
  11.0 1.3 convolution_add_fusion
  12.3 0.0 all-gather.10.cloned.1.call-update
  12.3 0.0 all-gather.6.cloned.1.call-start
  12.3 0.7 all-gather.6.cloned.1.call-update
  13.0 0.0 reduce-scatter.2.cloned.1.call-start
  13.1 0.0 copy-done.9
  13.1 0.6 dynamic-slice
  14.4 0.2 dynamic-update-slice
  14.6 132.0 %all-reduce = f32[512]{0:T(512)S(1)} all-reduce(f32[512]{0:T(512)S(1)} %dynamic-update-slice), channel_id=2, replica_groups=mesh['seq'=64,'pool'=4] {'seq'}, use_global_device_ids=true, to_apply=%add | all-reduce | flops 512 | bytes 4096
  146.6 0.1 reshape.211
  146.7 1.3 copy.51
  148.0 0.0 copy-done.6
  148.0 0.1 iota_compare_fusion
  148.1 10.6 %all-gather.10.cloned.1.call-done = f32[512,128,128]{2,1,0:T(8,128)} async-done(((f32[8,128,128]{2,1,0:T(8,128)}), f32[512,128,128]{2,1,0:T(8,128)}) %all-gather.10.cloned.1.call-update) | async-done | bytes 33554448 | tf_op jit(solution)/shard_map/all_gather | solution.py:13
  158.8 1.2 while.12
  158.8 1.2 bitcast_add_fusion.3
  160.0 0.0 copy-done
  160.0 2.4 fusion.11
  162.4 0.0 copy-start.4
  162.4 7.4 %fusion.5 = (f32[8,512]{1,0:T(8,128)S(1)}, f32[8,512,128]{1,2,0:T(8,128)}) fusion(f32[8,128,512]{2,1,0:T(8,128)} %fusion.11, f32[8,512]{1,0:T(8,128)S(1)} %get-tuple-element.62, bf16[8,512,128]{2,0,1:T(8,128)(2,1)} %bitcast.94, f32[8,512]{1,0:T(8,128)S(1)} %get-tuple-element.61, pred[512,512]{1,0:T(8,128)(4,1)S(1)} %iota_compare_fusion, ...), kind=kOutput, calls=%fused_computation.8 | convolution fusion | flops 1086320640 | bytes 7651328 | tf_op jit(solution)/shard_map/hij,hjd->hid/dot_general | solution.py:53
  169.9 0.0 copy-done.4
  169.9 2.2 fusion.8
  172.1 69.3 %all-gather.6.cloned.1.call-done = bf16[1024,4096]{0,1:T(8,128)(2,1)} async-done(((bf16[1024,64]{0,1:T(8,128)(2,1)}), bf16[1024,4096]{0,1:T(8,128)(2,1)}) %all-gather.6.cloned.1.call-update) | async-done | bytes 8388624 | tf_op jit(solution)/shard_map/all_gather | solution.py:91
  241.4 10.3 %fusion.25 = f32[512,4096]{1,0:T(8,128)} fusion(bf16[512,1024]{0,1:T(8,128)(2,1)S(1)} %bitcast.90, bf16[1024,4096]{0,1:T(8,128)(2,1)} %all-gather.6.cloned.1.call-done), kind=kOutput, calls=%fused_computation.50 | convolution fusion | flops 4294967296 | bytes 17825792 | tf_op jit(solution)/shard_map/dot_general | solution.py:89
  251.7 0.0 copy-start.8
  251.7 0.0 copy-start.3
  251.7 0.0 reduce-scatter.2.cloned.1.call-update
  251.7 0.0 copy-start.7
  251.7 0.0 all-gather.8.cloned.1.call-start
  251.8 0.5 all-gather.8.cloned.1.call-update
  252.3 0.0 copy-done.8
  252.4 0.6 fusion.24
  252.9 0.7 iota_compare_fusion.2
  253.6 0.7 iota_compare_fusion.1
  254.3 0.7 and_convert_fusion
  254.9 4.0 all-to-all-start
  258.9 78.1 %reduce-scatter.2.cloned.1.call-done = f32[128,4096]{1,0:T(8,128)} async-done(((f32[512,4096]{1,0:T(8,128)}), f32[128,4096]{1,0:T(8,128)}) %reduce-scatter.2.cloned.1.call-update) | async-done | bytes 2097168 | tf_op jit(solution)/shard_map/reduce_scatter | solution.py:94
  337.0 0.0 copy-done.3
  337.0 2.1 multiply_reduce_fusion
  339.1 83.8 %all-gather.8.cloned.1.call-done = bf16[4096,1024]{1,0:T(8,128)(2,1)} async-done(((bf16[64,1024]{1,0:T(8,128)(2,1)}), bf16[4096,1024]{1,0:T(8,128)(2,1)}) %all-gather.8.cloned.1.call-update) | async-done | bytes 8388624 | tf_op jit(solution)/shard_map/all_gather | solution.py:110
  422.9 0.0 copy-done.7
  422.9 0.0 copy-done.2
  422.9 4.7 %convolution_convert_fusion.1 = bf16[128,1024]{1,0:T(8,128)(2,1)S(1)} fusion(bf16[4096,1024]{1,0:T(8,128)(2,1)} %all-gather.8.cloned.1.call-done, f32[128,4096]{1,0:T(8,128)S(1)} %copy-done.2, bf16[128,4096]{1,0:T(8,128)(2,1)S(1)} %copy-done.3, f32[4096]{0:T(1024)S(1)} %copy-done.7, f32[128]{0:T(128)S(1)} %add_rsqrt_fusion), kind=kOutput, calls=%fused_computation.20 | convolution fusion | flops 1076494336 | bytes 11813376 | tf_op jit(solution)/shard_map/dot_general | solution.py:108
  427.6 0.0 copy-start.1
  427.6 1.1 broadcast_select_fusion
  428.8 0.0 all-to-all-done
  428.8 4.0 all-to-all-start.1
  432.7 0.1 copy.34
  432.8 14.5 %all-to-all-done.1 = bf16[4,1,128,1024]{3,2,1,0:T(8,128)(2,1)S(1)} async-done(((bf16[4,1,128,1024]{3,2,1,0:T(8,128)(2,1)}), bf16[4,1,128,1024]{3,2,1,0:T(8,128)(2,1)S(1)}, u32[]{:S(2)}, u32[]{:S(2)}) %all-to-all-start.1) | async-done | bytes 1048608 | tf_op jit(solution)/shard_map/all_to_all | solution.py:119
  447.4 0.9 fusion.9
  448.3 0.9 copy.42
  449.2 0.0 copy-done.1
  (9 shorter events, 0.1 us)
Async XLA Ops:
  6.5 153.5 %copy-start = (bf16[512,1024]{1,0:T(8,128)(2,1)S(1)}, bf16[512,1024]{1,0:T(8,128)(2,1)}, u32[]{:S(2)}) copy-start(bf16[512,1024]{1,0:T(8,128)(2,1)} %param.11) | copy-start | bytes 3145732
  6.5 4.4 copy-start.5
  6.5 152.2 %all-gather.10.cloned.1.call-start = ((), (), s32[]{:S(2)}) async-start(), calls=%async_computation.6 | async-start | bytes 34078720 | tf_op jit(solution)/shard_map/all_gather | solution.py:13
  11.0 137.1 %copy-start.6 = (bf16[512,1024]{0,1:T(8,128)(2,1)}, bf16[512,1024]{0,1:T(8,128)(2,1)S(1)}, u32[]{:S(2)}) copy-start(bf16[512,1024]{0,1:T(8,128)(2,1)S(1)} %copy.46) | copy-start | bytes 3145732
  11.0 2.1 copy-start.9
  12.3 229.1 %all-gather.6.cloned.1.call-start = ((), (), s32[]{:S(2)}) async-start(), calls=%async_computation.3 | async-start | bytes 8519680 | tf_op jit(solution)/shard_map/all_gather | solution.py:91
  13.0 324.0 %reduce-scatter.2.cloned.1.call-start = ((), (), s32[]{:S(2)}) async-start(), calls=%async_computation.4 | async-start | bytes 10485760 | tf_op jit(solution)/shard_map/reduce_scatter | solution.py:94
  162.4 7.5 %copy-start.4 = (f32[8,128,512]{2,1,0:T(8,128)S(1)}, f32[8,128,512]{2,1,0:T(8,128)}, u32[]{:S(2)}) copy-start(f32[8,128,512]{2,1,0:T(8,128)} %fusion.11) | copy-start | bytes 6291460
  251.7 0.7 copy-start.8
  251.7 85.3 %copy-start.3 = (bf16[128,4096]{1,0:T(8,128)(2,1)S(1)}, bf16[128,4096]{1,0:T(8,128)(2,1)}, u32[]{:S(2)}) copy-start(bf16[128,4096]{1,0:T(8,128)(2,1)} %param.15) | copy-start | bytes 3145732
  251.7 171.2 %copy-start.7 = (f32[4096]{0:T(1024)S(1)}, f32[4096]{0:T(1024)}, u32[]{:S(2)}) copy-start(f32[4096]{0:T(1024)} %param.17) | copy-start | bytes 49156
  251.7 171.2 %all-gather.8.cloned.1.call-start = ((), (), s32[]{:S(2)}) async-start(), calls=%async_computation.5 | async-start | bytes 8519680 | tf_op jit(solution)/shard_map/all_gather | solution.py:110
  254.9 173.8 %all-to-all-start = ((bf16[4,1,2]{2,1,0:T(2,128)(2,1)}), bf16[4,1,2]{2,1,0:T(2,128)(2,1)S(1)}, u32[]{:S(2)}, u32[]{:S(2)}) async-start(bf16[4,1,2]{2,1,0:T(2,128)(2,1)} %and_convert_fusion), calls=%async_computation | async-start | bytes 4096 | tf_op jit(solution)/shard_map/all_to_all | solution.py:120
  337.0 85.9 %copy-start.2 = (f32[128,4096]{1,0:T(8,128)S(1)}, f32[128,4096]{1,0:T(8,128)}, u32[]{:S(2)}) copy-start(f32[128,4096]{1,0:T(8,128)} %reduce-scatter.2.cloned.1.call-done) | copy-start | bytes 6291460
  427.6 21.6 %copy-start.1 = (bf16[512,1024]{1,0:T(8,128)(2,1)S(1)}, bf16[512,1024]{1,0:T(8,128)(2,1)}, u32[]{:S(2)}) copy-start(bf16[512,1024]{1,0:T(8,128)(2,1)} %param.11) | copy-start | bytes 3145732
  428.8 18.6 %all-to-all-start.1 = ((bf16[4,1,128,1024]{3,2,1,0:T(8,128)(2,1)}), bf16[4,1,128,1024]{3,2,1,0:T(8,128)(2,1)S(1)}, u32[]{:S(2)}, u32[]{:S(2)}) async-start(bf16[4,1,128,1024]{3,2,1,0:T(8,128)(2,1)} %broadcast_select_fusion), calls=%async_computation.2 | async-start | bytes 2097152 | tf_op jit(solution)/shard_map/all_to_all | solution.py:119
Sparse Core Ops, SparseCore 0:
  12.4 146.2 all-gather.9
  161.5 79.8 all-gather.5
  251.9 85.1 reduce-scatter.1
  339.7 83.2 all-gather.7
where the time goes:
time: 459 us; the launch traced here: 456 us
  waiting for transfers between devices  258 us (56%)
  blocking collectives  132 us (29%)
  matrix products  27 us (6%)
  between operations  13.9 us (3%)
  other arithmetic  11.2 us (2%)
  starting transfers between devices  8.06 us (2%)
  local copies, waits for them, and re-layouts  5.81 us (1%)
    unnamed x1, blocking collectives  132 us
    all_gather x1, waiting for transfers between devices, on_device(): lax.all_gather(kv_weight, 'seq', axis=0, tiled=True)  83.8 us
    reduce_scatter x1, waiting for transfers between devices, on_device(): lax.psum_scatter(partial_value, 'pool', scatter_dimension=0, tiled=True)  78.1 us
    all_gather x1, waiting for transfers between devices, on_device(): lax.all_gather(out_weight, 'seq', axis=1, tiled=True)  69.3 us
    all_to_all x1, waiting for transfers between devices, on_device(): lax.all_to_all(outgoing, 'pool', split_axis=0, concat_axis=0, tiled=True)  14.5 us
    all_gather x1, waiting for transfers between devices, entering(): gathered = jax.tree.map(lambda a: lax.all_gather(a, axis), part)  10.6 us
    dot_general x1, matrix products, on_device(): jnp.dot(mixed_list, lax.all_gather(out_weight, 'seq', axis=1, tiled=True)...  10.3 us
  transfers between devices with their start and end apart: 6, of which 5 were waited for; matrix products, arithmetic and copies ran while one was open for 6% of the time, Pallas kernels for 0%

commit v1 on v0

--- a/solution.py
+++ b/solution.py
@@ -6,6 +6,9 @@
 HD = 128
 PAGE = 128
 BLK = 512
+state_values = lambda panel, pos_dim: jnp.concatenate(
+    lax.all_to_all(jnp.stack([panel for _ in range(lax.psum(1, "seq"))]), "seq", 0, 0), axis=pos_dim
+)
 
 
 def entering(part, axis, combine, identity):
@@ -87,9 +90,7 @@
     scaled = retained * lax.rsqrt(jnp.mean(retained * retained, axis=-1, keepdims=True) + 1e-05)
     mixed_list = scaled.transpose(1, 0, 2).reshape(BLK, head_count * HD).astype(jnp.bfloat16)
     partial_value = jnp.dot(
-        mixed_list,
-        lax.all_gather(out_weight, "seq", axis=1, tiled=True),
-        preferred_element_type=jnp.float32,
+        mixed_list, state_values(out_weight, 1), preferred_element_type=jnp.float32
     )
     summed = lax.psum_scatter(partial_value, "pool", scatter_dimension=0, tiled=True)
     hidden = residual.astype(jnp.float32) + summed

time: 459 us -> 706 us (1.54)
  blocking collectives: 132 us -> 371 us
  starting transfers between devices: 8.06 us -> 21.7 us
  waiting for transfers between devices: 258 us -> 248 us
    unnamed x1, blocking collectives: 132 us -> 371 us
    reduce_scatter x1, waiting for transfers between devices: 78.1 us -> 148 us  [on_device(): lax.psum_scatter(partial_value, 'pool', scatter_dimension=0, tiled=True)]
    all_gather x1 -> x0, waiting for transfers between devices: 69.3 us -> none  [on_device(): lax.all_gather(out_weight, 'seq', axis=1, tiled=True)]
    all_to_all x0 -> x1, starting transfers between devices: none -> 13.5 us  [lax.all_to_all(jnp.stack([panel for _ in range(lax.psum(1, 'seq'))]), 'se...]
    all_gather x1, waiting for transfers between devices: 10.6 us -> 0.02 us  [entering(): gathered = jax.tree.map(lambda a: lax.all_gather(a, axis), part)]
  transfers between devices with their start and end apart: 6 -> 6, of which waited for: 5 -> 3; matrix products, arithmetic and copies ran while one was open for 6% -> 4% of each run, Pallas kernels for 0% -> 0%
where the time goes in v1:
time: 706 us; the launch traced here: 702 us
  blocking collectives  371 us (53%)
  waiting for transfers between devices  248 us (35%)
  matrix products  27 us (4%)
  starting transfers between devices  21.7 us (3%)
  between operations  14 us (2%)
  other arithmetic  11.2 us (2%)
  local copies, waits for them, and re-layouts  10.1 us (1%)
    unnamed x1, blocking collectives  371 us
    reduce_scatter x1, waiting for transfers between devices, on_device(): lax.psum_scatter(partial_value, 'pool', scatter_dimension=0, tiled=True)  148 us
    all_gather x1, waiting for transfers between devices, on_device(): lax.all_gather(kv_weight, 'seq', axis=0, tiled=True)  84 us
    all_to_all x1, waiting for transfers between devices, on_device(): lax.all_to_all(outgoing, 'pool', split_axis=0, concat_axis=0, tiled=True)  14.5 us
  transfers between devices with their start and end apart: 6, of which 3 were waited for; matrix products, arithmetic and copies ran while one was open for 4% of the time, Pallas kernels for 0%

profile of v1, /device:TPU:1, one launch (start us, length us, event | category | flops | bytes accessed | tf_op | source)
XLA Modules:
  0.0 702.2 jit_solution(15287521809159446918)
XLA Ops:
  6.5 0.0 copy-start
  6.5 0.0 copy-start.5
  6.5 0.0 all-gather.7.cloned.1.call-start
  6.5 2.4 reduce-window.6
  8.9 0.2 slice_reduce_fusion
  9.1 0.1 exponential_bitcast_fusion.1
  9.2 0.2 slice_reduce_fusion.1
  9.4 0.1 fusion.23
  9.5 1.5 copy.47
  11.0 0.0 copy-start.6
  11.0 0.0 copy-start.7
  11.0 0.0 copy-done.5
  11.0 1.3 convolution_add_fusion
  12.3 0.0 all-gather.7.cloned.1.call-update
  12.3 0.0 copy-done.7
  12.3 4.3 stack.2
  16.6 0.0 copy-done.6
  16.6 0.0 copy-start.10
  16.6 13.5 %all-to-all-start.1 = ((bf16[64,1024,64]{1,2,0:T(8,128)(2,1)}), bf16[64,1024,64]{1,2,0:T(8,128)(2,1)}, u32[]{:S(2)}, u32[]{:S(2)}) async-start(bf16[64,1024,64]{1,2,0:T(8,128)(2,1)} %stack.2), calls=%async_computation.1 | async-start | bytes 16777216 | tf_op jit(solution)/shard_map/all_to_all | solution.py:10
  30.1 0.0 reduce-scatter.2.cloned.1.call-start
  30.1 0.0 copy-done.10
  30.1 0.6 dynamic-slice
  31.4 0.2 dynamic-update-slice
  31.6 370.7 %all-reduce = f32[512]{0:T(512)S(1)} all-reduce(f32[512]{0:T(512)S(1)} %dynamic-update-slice), channel_id=2, replica_groups=mesh['seq'=64,'pool'=4] {'seq'}, use_global_device_ids=true, to_apply=%add | all-reduce | flops 512 | bytes 4096
  402.3 0.1 reshape.221
  402.4 1.3 copy.52
  403.7 0.1 iota_compare_fusion
  403.8 0.0 all-gather.7.cloned.1.call-done
  403.8 1.2 while.12
  403.9 1.2 bitcast_add_fusion.3
  405.1 0.0 copy-done
  405.1 2.4 fusion.11
  407.5 0.0 copy-start.4
  407.5 7.4 %fusion.5 = (f32[8,512]{1,0:T(8,128)S(1)}, f32[8,512,128]{1,2,0:T(8,128)}) fusion(f32[8,128,512]{2,1,0:T(8,128)} %fusion.11, f32[8,512]{1,0:T(8,128)S(1)} %get-tuple-element.62, bf16[8,512,128]{2,0,1:T(8,128)(2,1)} %bitcast.97, f32[8,512]{1,0:T(8,128)S(1)} %get-tuple-element.61, pred[512,512]{1,0:T(8,128)(4,1)S(1)} %iota_compare_fusion, ...), kind=kOutput, calls=%fused_computation.8 | convolution fusion | flops 1086320640 | bytes 7651328 | tf_op jit(solution)/shard_map/hij,hjd->hid/dot_general | solution.py:56
  414.9 0.0 copy-done.4
  415.0 2.2 fusion.8
  417.1 0.0 all-to-all-done.1
  417.1 10.3 %fusion.25 = f32[512,4096]{1,0:T(8,128)} fusion(bf16[512,1024]{0,1:T(8,128)(2,1)S(1)} %bitcast.93, bf16[1024,4096]{0,1:T(8,128)(2,1)} %bitcast.23), kind=kOutput, calls=%fused_computation.50 | convolution fusion | flops 4294967296 | bytes 17825792 | tf_op jit(solution)/shard_map/dot_general | solution.py:92
  427.4 0.0 reduce-scatter.2.cloned.1.call-update
  427.5 0.0 copy-start.8
  427.5 0.0 all-gather.5.cloned.1.call-start
  427.5 0.7 all-gather.5.cloned.1.call-update
  428.2 0.0 copy-done.9
  428.2 0.6 fusion.24
  428.8 0.7 iota_compare_fusion.2
  429.5 0.7 iota_compare_fusion.1
  430.2 0.7 and_convert_fusion
  430.8 4.2 all-to-all-start
  435.0 148.4 %reduce-scatter.2.cloned.1.call-done = f32[128,4096]{1,0:T(8,128)} async-done(((f32[512,4096]{1,0:T(8,128)}), f32[128,4096]{1,0:T(8,128)}) %reduce-scatter.2.cloned.1.call-update) | async-done | bytes 2097168 | tf_op jit(solution)/shard_map/reduce_scatter | solution.py:95
  583.4 0.0 copy-done.3
  583.4 2.1 multiply_reduce_fusion
  585.5 84.0 %all-gather.5.cloned.1.call-done = bf16[4096,1024]{1,0:T(8,128)(2,1)} async-done(((bf16[64,1024]{1,0:T(8,128)(2,1)}), bf16[4096,1024]{1,0:T(8,128)(2,1)}) %all-gather.5.cloned.1.call-update) | async-done | bytes 8388624 | tf_op jit(solution)/shard_map/all_gather | solution.py:111
  669.4 0.0 copy-done.8
  669.4 0.0 copy-done.2
  669.4 4.7 convolution_convert_fusion.1
  674.1 0.0 copy-start.1
  674.1 1.1 broadcast_select_fusion
  675.2 0.0 all-to-all-done
  675.2 4.0 all-to-all-start.2
  679.2 0.1 copy.35
  679.3 14.5 %all-to-all-done.2 = bf16[4,1,128,1024]{3,2,1,0:T(8,128)(2,1)S(1)} async-done(((bf16[4,1,128,1024]{3,2,1,0:T(8,128)(2,1)}), bf16[4,1,128,1024]{3,2,1,0:T(8,128)(2,1)S(1)}, u32[]{:S(2)}, u32[]{:S(2)}) %all-to-all-start.2) | async-done | bytes 1048608 | tf_op jit(solution)/shard_map/all_to_all | solution.py:120
  693.9 0.9 fusion.9
  694.8 0.9 copy.43
  695.7 0.0 copy-done.1
  (11 shorter events, 0.1 us)
Async XLA Ops:
  6.5 398.6 %copy-start = (bf16[512,1024]{1,0:T(8,128)(2,1)S(1)}, bf16[512,1024]{1,0:T(8,128)(2,1)}, u32[]{:S(2)}) copy-start(bf16[512,1024]{1,0:T(8,128)(2,1)} %param.11) | copy-start | bytes 3145732
  6.5 4.4 copy-start.5
  6.5 397.3 %all-gather.7.cloned.1.call-start = ((), (), s32[]{:S(2)}) async-start(), calls=%async_computation.6 | async-start | bytes 34078720 | tf_op jit(solution)/shard_map/all_gather | solution.py:16
  11.0 5.6 copy-start.6
  11.0 1.3 copy-start.7
  16.6 13.5 %copy-start.10 = (u32[256]{0:T(256)S(1)}, u32[256]{0:T(256)}, u32[]{:S(2)}) copy-start(u32[256]{0:T(256)} %constant.48) | copy-start | bytes 3076
  16.6 400.5 %all-to-all-start.1 = ((bf16[64,1024,64]{1,2,0:T(8,128)(2,1)}), bf16[64,1024,64]{1,2,0:T(8,128)(2,1)}, u32[]{:S(2)}, u32[]{:S(2)}) async-start(bf16[64,1024,64]{1,2,0:T(8,128)(2,1)} %stack.2), calls=%async_computation.1 | async-start | bytes 16777216 | tf_op jit(solution)/shard_map/all_to_all | solution.py:10
  30.1 553.3 %reduce-scatter.2.cloned.1.call-start = ((), (), s32[]{:S(2)}) async-start(), calls=%async_computation.4 | async-start | bytes 10485760 | tf_op jit(solution)/shard_map/reduce_scatter | solution.py:95
  407.5 7.5 %copy-start.4 = (f32[8,128,512]{2,1,0:T(8,128)S(1)}, f32[8,128,512]{2,1,0:T(8,128)}, u32[]{:S(2)}) copy-start(f32[8,128,512]{2,1,0:T(8,128)} %fusion.11) | copy-start | bytes 6291460
  427.4 0.8 copy-start.9
  427.4 155.9 %copy-start.3 = (bf16[128,4096]{1,0:T(8,128)(2,1)S(1)}, bf16[128,4096]{1,0:T(8,128)(2,1)}, u32[]{:S(2)}) copy-start(bf16[128,4096]{1,0:T(8,128)(2,1)} %param.15) | copy-start | bytes 3145732
  427.5 242.0 %copy-start.8 = (f32[4096]{0:T(1024)S(1)}, f32[4096]{0:T(1024)}, u32[]{:S(2)}) copy-start(f32[4096]{0:T(1024)} %param.17) | copy-start | bytes 49156
  427.5 241.9 %all-gather.5.cloned.1.call-start = ((), (), s32[]{:S(2)}) async-start(), calls=%async_computation.5 | async-start | bytes 8519680 | tf_op jit(solution)/shard_map/all_gather | solution.py:111
  430.8 244.4 %all-to-all-start = ((bf16[4,1,2]{2,1,0:T(2,128)(2,1)}), bf16[4,1,2]{2,1,0:T(2,128)(2,1)S(1)}, u32[]{:S(2)}, u32[]{:S(2)}) async-start(bf16[4,1,2]{2,1,0:T(2,128)(2,1)} %and_convert_fusion), calls=%async_computation | async-start | bytes 4096 | tf_op jit(solution)/shard_map/all_to_all | solution.py:121
  583.4 86.1 %copy-start.2 = (f32[128,4096]{1,0:T(8,128)S(1)}, f32[128,4096]{1,0:T(8,128)}, u32[]{:S(2)}) copy-start(f32[128,4096]{1,0:T(8,128)} %reduce-scatter.2.cloned.1.call-done) | copy-start | bytes 6291460
  674.1 21.6 %copy-start.1 = (bf16[512,1024]{1,0:T(8,128)(2,1)S(1)}, bf16[512,1024]{1,0:T(8,128)(2,1)}, u32[]{:S(2)}) copy-start(bf16[512,1024]{1,0:T(8,128)(2,1)} %param.11) | copy-start | bytes 3145732
  675.2 18.6 %all-to-all-start.2 = ((bf16[4,1,128,1024]{3,2,1,0:T(8,128)(2,1)}), bf16[4,1,128,1024]{3,2,1,0:T(8,128)(2,1)S(1)}, u32[]{:S(2)}, u32[]{:S(2)}) async-start(bf16[4,1,128,1024]{3,2,1,0:T(8,128)(2,1)} %broadcast_select_fusion), calls=%async_computation.3 | async-start | bytes 2097152 | tf_op jit(solution)/shard_map/all_to_all | solution.py:120
Sparse Core Ops, SparseCore 0:
  12.4 302.3 all-gather.6
  427.6 155.7 reduce-scatter.1
  586.1 83.2 all-gather.4
